TPU v7x, 32 devices: a whole 2x2x4 slice. The times are simulated.
32 devices in a mesh: tm: 2 (over y), pairs: 16 (over z, x, core).
Axes of the slice: x: 2, y: 2, z: 4, core: 2. Of those that a mesh axis runs over, the one named last changes fastest.
Arguments:
- records: bfloat16 [2, 512, 128, 2048], P('tm', 'pairs')
- source_map: int32 [2, 512], P('tm'), may hold values from 0 to 511, each once within a row
- pair_blocks: int32 [16, 6, 2], P('pairs'), may hold values from -1 to 31, as said below
Outputs:
- stacks: float32 [96, 16, 2, 128, 128], P('pairs', 'tm')
Inputs may be any that keep to these rules, and one draw needn't show every extreme that they name: `pair_blocks`: each pair slot holds blocks i <= j with j - i <= 2, or -1 and -1 when empty; every such pair appears in exactly one slot; some owner has all 6 slots filled. `source_map`: each row is a permutation: every slot of a time group holds exactly one window of one channel block.
All inputs are finite; a program needn't handle non-finite values.
Results may differ from a plain program's by a relative error of at most 0.0056.
Values may be sent and summed in bfloat16 or wider, within the bound.
A program may use at most 128 MiB of HBM per device.

v0:
```python
import math

import jax
import jax.numpy as jnp
from jax import lax
from jax.sharding import PartitionSpec as P

NB = 32
BINS = 16
FIRST_BIN = 64
WIN = 16


def transform_table(length):
    samples = jnp.arange(length, dtype=jnp.int32)
    bin_index = FIRST_BIN + jnp.arange(BINS, dtype=jnp.int32)
    phases = samples[:, None] * bin_index[None, :] % length
    angles = 2.0 * math.pi / length * phases.astype(jnp.float32)
    taper = 0.5 - 0.5 * jnp.cos(2.0 * math.pi / length * samples.astype(jnp.float32))
    weight_col = (taper / math.sqrt(length))[:, None]
    return jnp.concatenate(
        [jnp.cos(angles) * weight_col, -jnp.sin(angles) * weight_col], axis=1
    ).astype(jnp.bfloat16)


def whiten_spectra(windows, table):
    transformed = jnp.einsum("scn,nk->skc", windows, table, preferred_element_type=jnp.float32)
    real_part = transformed[:, :BINS]
    imag_part = transformed[:, BINS:]
    power = jnp.mean(real_part * real_part + imag_part * imag_part, axis=2, keepdims=True)
    inverse = 1.0 / jnp.sqrt(power + 1e-06)
    return (transformed * jnp.concatenate([inverse, inverse], axis=1)).astype(jnp.bfloat16)


def cross_stack(left_spec, right_spec):
    real_sum = jnp.einsum(
        "pwfi,pwfj->pfij",
        left_spec[:, :, 0],
        right_spec[:, :, 0],
        preferred_element_type=jnp.float32,
    )
    real_sum = real_sum + jnp.einsum(
        "pwfi,pwfj->pfij",
        left_spec[:, :, 1],
        right_spec[:, :, 1],
        preferred_element_type=jnp.float32,
    )
    imag_sum = jnp.einsum(
        "pwfi,pwfj->pfij",
        left_spec[:, :, 1],
        right_spec[:, :, 0],
        preferred_element_type=jnp.float32,
    )
    imag_sum = imag_sum - jnp.einsum(
        "pwfi,pwfj->pfij",
        left_spec[:, :, 0],
        right_spec[:, :, 1],
        preferred_element_type=jnp.float32,
    )
    return jnp.stack([real_sum, imag_sum], axis=2)


def per_device(records, source_map, pair_blocks):
    table = transform_table(records.shape[3])
    local_spec = whiten_spectra(records[0], table)
    channels = local_spec.shape[2]
    blocks = pair_blocks[0]
    slot_count = blocks.shape[0]
    valid = (blocks[:, 0] >= 0).astype(jnp.float32)
    safe_blocks = jnp.maximum(blocks, 0)
    window_ids = jnp.arange(WIN, dtype=jnp.int32)
    columns = window_ids[None, None, :] * NB + safe_blocks[:, :, None]
    wanted = jnp.take(source_map[0], columns.reshape(-1))
    piece = lax.all_gather(local_spec, "pairs", axis=0, tiled=True)
    row_ids = jnp.arange(piece.shape[0], dtype=jnp.int32)
    onehot = (wanted[:, None] == row_ids[None, :]).astype(jnp.bfloat16)
    collected = jnp.einsum("nr,rkc->nkc", onehot, piece, preferred_element_type=jnp.float32)
    picked = collected.astype(jnp.bfloat16)
    chosen = picked.reshape(slot_count, 2, WIN, 2, BINS, channels)
    norm_factor = 1.0 / math.sqrt(WIN * lax.axis_size("tm"))
    partial_stack = cross_stack(chosen[:, 0], chosen[:, 1])
    summed = lax.psum_scatter(partial_stack, "tm", scatter_dimension=1, tiled=True)
    return summed * (valid * norm_factor)[:, None, None, None, None]


def solution(mesh):
    return jax.shard_map(
        per_device,
        mesh=mesh,
        in_specs=(P("tm", "pairs", None, None), P("tm", None), P("pairs", None, None)),
        out_specs=P("pairs", "tm", None, None, None),
        check_vma=False,
    )
```

profile of v0, /device:TPU:0, one launch (start us, length us, event | category | flops | bytes accessed | tf_op | source)
XLA Modules:
  0.0 275.5 jit_solution(10862450789281669629)
XLA Ops:
  6.6 0.6 multiply_convert_fusion.2
  7.2 8.6 %fusion.7 = f32[32,32,128]{2,1,0:T(8,128)S(1)} fusion(bf16[1,32,128,2048]{3,2,1,0:T(8,128)(2,1)} %param.3, bf16[2048,16]{0,1:T(8,128)(2,1)S(1)} %get-tuple-element.8, bf16[2048,16]{0,1:T(8,128)(2,1)S(1)} %get-tuple-element.7), kind=kOutput, calls=%fused_computation.11 | convolution fusion | flops 537133056 | bytes 17432576 | tf_op jit(solution)/shard_map/scn,nk->skc/dot_general | solution.py:27
  15.8 0.2 fusion.15
  16.0 0.1 maximum_bitcast_fusion.2
  16.1 0.9 multiply_convert_fusion
  17.1 0.1 copy.14
  17.2 0.1 add.102
  17.3 0.1 add.99
  17.4 1.8 gather_fusion
  19.2 51.1 %all-gather.2.cloned.1.call-done = bf16[512,32,128]{2,1,0:T(8,128)(2,1)} async-done(((bf16[32,32,128]{2,1,0:T(8,128)(2,1)}), bf16[512,32,128]{2,1,0:T(8,128)(2,1)}) %all-gather.2.cloned.1.call-update) | async-done | bytes 4194320 | tf_op jit(solution)/shard_map/all_gather | solution.py:74
  70.4 4.0 %fusion.4 = bf16[192,32,128]{2,0,1:T(8,128)(2,1)S(1)} fusion(bf16[512,32,128]{2,1,0:T(8,128)(2,1)} %all-gather.2.cloned.1.call-done, s32[192]{0:T(256)S(1)} %and_select_fusion), kind=kOutput, calls=%fused_computation.10 | convolution fusion | flops 806191104 | bytes 5767936 | tf_op jit(solution)/shard_map/nr,rkc->nkc/dot_general | solution.py:77
  74.4 0.3 fusion.27
  74.7 0.4 copy_bitcast_fusion.1
  75.1 1.0 fusion.12
  76.1 1.0 fusion.13
  77.1 1.0 add_bitcast_fusion
  78.2 3.7 %subtract_bitcast_fusion = f32[6,16,1,128,128]{4,3,1,0,2:T(8,128)} fusion(f32[6,16,128,128]{3,2,1,0:T(8,128)S(1)} %fusion.13, bf16[6,16,2,16,128]{4,1,3,0,2:T(8,128)(2,1)S(1)} %get-tuple-element.10, bf16[6,16,2,16,128]{4,1,3,0,2:T(8,128)(2,1)S(1)} %get-tuple-element.9), kind=kOutput, calls=%fused_computation.6 | convolution fusion | flops 51904512 | bytes 13369344 | tf_op jit(solution)/shard_map/pwfi,pwfj->pfij/dot_general | solution.py:54
  81.9 9.6 %pad_maximum_fusion = f32[6,16,2,128,128]{4,3,1,0,2:T(8,128)} fusion(f32[6,16,1,128,128]{4,3,1,0,2:T(8,128)} %subtract_bitcast_fusion, f32[6,16,1,128,128]{4,3,1,0,2:T(8,128)S(1)} %add_bitcast_fusion), kind=kLoop, calls=%fused_computation.4 | loop fusion | flops 3145728 | bytes 25165824 | tf_op jit(solution)/shard_map/stack | solution.py:60
  91.5 11.3 %copy.19 = f32[6,16,2,128,128]{4,3,0,2,1:T(8,128)} copy(f32[6,16,2,128,128]{4,3,1,0,2:T(8,128)} %pad_maximum_fusion) | data formatting | bytes 25165824
  102.8 14.4 %copy.33 = f32[2,8,1536,128]{3,1,2,0:T(8,128)} copy(f32[2,8,1536,128]{3,2,1,0:T(8,128)} %bitcast.64) | data formatting | bytes 25165824
  117.2 143.1 %reduce-scatter.5.cloned.1.call-done = f32[8,196608]{1,0:T(8,128)} async-done(((f32[16,196608]{1,0:T(8,128)}), f32[8,196608]{1,0:T(8,128)}) %reduce-scatter.5.cloned.1.call-update) | async-done | bytes 6291472
  260.4 4.0 %copy.24 = f32[1,8,1536,128]{3,2,1,0:T(8,128)S(1)} copy(f32[1,8,1536,128]{3,1,2,0:T(8,128)} %bitcast.66) | data formatting | bytes 12582912
  264.4 1.1 copy_multiply_fusion
  265.5 3.1 %copy.18 = f32[6,8,2,128,128]{4,3,2,1,0:T(8,128)} copy(f32[6,8,2,128,128]{4,3,1,0,2:T(8,128)S(1)} %copy_multiply_fusion) | data formatting | bytes 12582912 | tf_op jit(solution)/shard_map/mul | solution.py:83
  (20 shorter events, 0.3 us)
Async XLA Ops:
  6.5 10.9 %copy-start = (s32[1,512]{1,0:T(1,128)S(1)}, s32[1,512]{1,0:T(1,128)}, u32[]{:S(2)}) copy-start(s32[1,512]{1,0:T(1,128)} %param.4) | copy-start | bytes 6148
  6.5 63.9 %all-gather.2.cloned.1.call-start = ((), (), s32[]{:S(2)}) async-start(), calls=%async_computation.1 | async-start | bytes 4456448 | tf_op jit(solution)/shard_map/all_gather | solution.py:74
  7.2 9.8 %copy-start.2 = (s32[1,6,2]{1,2,0:T(2,128)S(1)}, s32[1,6,2]{1,2,0:T(2,128)}, u32[]{:S(2)}) copy-start(s32[1,6,2]{1,2,0:T(2,128)} %param.5) | copy-start | bytes 148
  17.0 243.4 %reduce-scatter.5.cloned.1.call-start = ((), (), s32[]{:S(2)}) async-start(), calls=%async_computation.2 | async-start | bytes 18874368
  264.4 4.3 %copy-start.1 = (s32[1,512]{1,0:T(1,128)S(1)}, s32[1,512]{1,0:T(1,128)}, u32[]{:S(2)}) copy-start(s32[1,512]{1,0:T(1,128)} %param.4) | copy-start | bytes 6148
Sparse Core Ops, SparseCore 0:
  17.1 53.2 all-gather.1
  117.3 142.9 reduce-scatter.4
where the time goes:
time: 276 us
  waiting for transfers between devices  194 us (70%)
  local copies, waits for them, and re-layouts  35.6 us (13%)
  matrix products  19.3 us (7%)
  between operations  13.6 us (5%)
  other arithmetic  12.7 us (5%)
    unnamed x3, waiting for transfers between devices  143 us
    all_gather x1, waiting for transfers between devices, per_device(): piece = lax.all_gather(local_spec, 'pairs', axis=0, tiled=True)  51.1 us
    unnamed x9, local copies, waits for them, and re-layouts  29.7 us
    another operation x1, other arithmetic, cross_stack(): return jnp.stack([real_sum, imag_sum], axis=2)  9.6 us
    dot_general x1, matrix products, whiten_spectra(): jnp.einsum('scn,nk->skc', windows, table, preferred_element_type=jnp.floa...  8.57 us
  transfers between devices with their start and end apart: 2, of which 2 were waited for; matrix products, arithmetic and copies ran while one was open for 1% of the time, Pallas kernels for 0%

commit v1 on v0

v1 whole, which is shorter than its diff:
```python
import functools
import math

import jax
import jax.numpy as jnp
import numpy as np
from jax import lax
from jax.experimental import pallas as pl
from jax.experimental.pallas import tpu as pltpu
from jax.sharding import PartitionSpec as P

NB = 32
BINS = 16
FIRST_BIN = 64
WIN = 16
MESH = pl.DeviceIdType.MESH


def transform_table(length):
    samples = jnp.arange(length, dtype=jnp.int32)
    bin_index = FIRST_BIN + jnp.arange(BINS, dtype=jnp.int32)
    phases = samples[:, None] * bin_index[None, :] % length
    angles = 2.0 * math.pi / length * phases.astype(jnp.float32)
    taper = 0.5 - 0.5 * jnp.cos(2.0 * math.pi / length * samples.astype(jnp.float32))
    weight_col = (taper / math.sqrt(length))[:, None]
    return jnp.concatenate(
        [jnp.cos(angles) * weight_col, -jnp.sin(angles) * weight_col], axis=1
    ).astype(jnp.bfloat16)


def whiten_spectra(windows, table):
    transformed = jnp.einsum("scn,nk->skc", windows, table, preferred_element_type=jnp.float32)
    real_part = transformed[:, :BINS]
    imag_part = transformed[:, BINS:]
    power = jnp.mean(real_part * real_part + imag_part * imag_part, axis=2, keepdims=True)
    inverse = 1.0 / jnp.sqrt(power + 1e-06)
    return (transformed * jnp.concatenate([inverse, inverse], axis=1)).astype(jnp.bfloat16)


def exchange_kernel(groups, pairs, own_ref, map_ref, out_ref, maps_ref,
                    send_sems, recv_sems, tm_send, map_send, map_recv, local_sems):
    depth = pairs // 4
    t = lax.axis_index("tm")
    me = lax.axis_index("pairs")
    z = me // 4
    x = (me // 2) % 2
    c = me % 2

    def slot(zz, xx, cc):
        return zz * 4 + xx * 2 + cc

    up, down = me + 4, me - 4
    side = slot(z, 1 - x, c)
    twin = slot(z, x, 1 - c)
    has_up = z < depth - 1
    has_down = z > 0

    barrier = pltpu.get_barrier_semaphore()
    for d in range(1, groups):
        pl.semaphore_signal(barrier, inc=1, device_id=((t + d) % groups, me), device_id_type=MESH)
    for other in (side, twin):
        pl.semaphore_signal(barrier, inc=1, device_id=(t, other), device_id_type=MESH)

    @pl.when(has_up)
    def _():
        pl.semaphore_signal(barrier, inc=1, device_id=(t, up), device_id_type=MESH)

    @pl.when(has_down)
    def _():
        pl.semaphore_signal(barrier, inc=1, device_id=(t, down), device_id_type=MESH)

    pl.semaphore_wait(barrier, groups + 1 + has_up.astype(jnp.int32) + has_down.astype(jnp.int32))

    def send(way, group, place, target, source=None):
        piece = out_ref.at[group, place]
        return pltpu.make_async_remote_copy(
            src_ref=piece if source is None else source,
            dst_ref=piece,
            send_sem=send_sems.at[way, group, place],
            recv_sem=recv_sems.at[group, place],
            device_id=(t, target),
            device_id_type=MESH,
        )

    def arrived(group, place):
        pltpu.make_async_copy(
            out_ref.at[group, place], out_ref.at[group, place], recv_sems.at[group, place]
        ).wait()

    def tm_copy(d):
        peer = (t + d) % groups
        return pltpu.make_async_remote_copy(
            src_ref=own_ref.at[peer],
            dst_ref=out_ref.at[t, me],
            send_sem=tm_send.at[d],
            recv_sem=recv_sems.at[t, me],
            device_id=(peer, me),
            device_id_type=MESH,
        )

    def map_copy(d):
        peer = (t + d) % groups
        return pltpu.make_async_remote_copy(
            src_ref=map_ref.at[0],
            dst_ref=maps_ref.at[t],
            send_sem=map_send.at[d],
            recv_sem=map_recv.at[t],
            device_id=(peer, me),
            device_id_type=MESH,
        )

    for d in range(1, groups):
        tm_copy(d).start()
        map_copy(d).start()
    keep = pltpu.make_async_copy(own_ref.at[t], out_ref.at[t, me], local_sems.at[0])
    keep.start()
    keep_map = pltpu.make_async_copy(map_ref.at[0], maps_ref.at[t], local_sems.at[1])
    keep_map.start()

    def spread(group, place, source, upward, downward):
        if upward is not None:
            @pl.when(upward)
            def _():
                send(0, group, place, up, source).start()
        if downward is not None:
            @pl.when(downward)
            def _():
                send(1, group, place, down, source).start()
        send(2, group, place, side, source).start()
        send(3, group, place, twin, source).start()

    order = [(t + d) % groups for d in range(groups)]
    for d, group in enumerate(order):
        if d:
            arrived(group, me)
        spread(group, me, None if d else own_ref.at[t], has_up, has_down)

    def side_arrivals(step):
        for group in order:
            for sign in ((1, -1) if step else (0,)):
                where = z + sign * step

                @pl.when((where >= 0) & (where < depth))
                def _():
                    place = slot(where, 1 - x, c)
                    arrived(group, place)
                    send(3, group, place, twin).start()

    for step in range(1, depth):
        for group in order:
            @pl.when(z - step >= 0)
            def _():
                place = slot(z - step, x, c)
                arrived(group, place)
                spread(group, place, None, has_up, None)

            @pl.when(z + step < depth)
            def _():
                place = slot(z + step, x, c)
                arrived(group, place)
                spread(group, place, None, None, has_down)
        if step >= 2:
            side_arrivals(step - 2)
    for step in range(max(depth - 2, 0), depth):
        side_arrivals(step)

    keep.wait()
    keep_map.wait()
    for d in range(1, groups):
        tm_copy(d).wait_send()
        map_copy(d).wait_send()
        pltpu.make_async_copy(
            maps_ref.at[order[d]], maps_ref.at[order[d]], map_recv.at[order[d]]
        ).wait()
    for group in order:
        for zz in range(depth):
            for xx in range(2):
                arrived(group, slot(zz, xx, 1 - c))
    for group in order:
        for zz in range(depth):
            place = slot(zz, x, c)

            @pl.when(has_up & (zz <= z))
            def _():
                send(0, group, place, up).wait_send()

            @pl.when(has_down & (zz >= z))
            def _():
                send(1, group, place, down).wait_send()

            send(2, group, place, side).wait_send()
            send(3, group, place, twin).wait_send()
            send(3, group, slot(zz, 1 - x, c), twin).wait_send()


def exchange(own, local_map, groups, pairs):
    _, rows, width = own.shape
    return pl.pallas_call(
        functools.partial(exchange_kernel, groups, pairs),
        out_shape=(
            jax.ShapeDtypeStruct((groups, pairs, rows, width), own.dtype),
            jax.ShapeDtypeStruct((groups,) + local_map.shape[1:], local_map.dtype),
        ),
        in_specs=[pl.BlockSpec(memory_space=pl.ANY)] * 2,
        out_specs=(pl.BlockSpec(memory_space=pl.ANY),) * 2,
        scratch_shapes=[
            pltpu.SemaphoreType.DMA((4, groups, pairs)),
            pltpu.SemaphoreType.DMA((groups, pairs)),
            pltpu.SemaphoreType.DMA((groups,)),
            pltpu.SemaphoreType.DMA((groups,)),
            pltpu.SemaphoreType.DMA((groups,)),
            pltpu.SemaphoreType.DMA((2,)),
        ],
        compiler_params=pltpu.CompilerParams(collective_id=0, has_side_effects=True),
        name="exchange",
    )(own, local_map)


def stack_kernel(groups, slots, bins, channels, scale, blocks_ref, maps_ref, spectra_ref, out_ref, picked):
    s = pl.program_id(0)
    items = spectra_ref.shape[1]

    @pl.when(s == 0)
    def _():
        lanes = lax.broadcasted_iota(jnp.int32, (WIN, NB), 1)
        rows = lax.broadcasted_iota(jnp.int32, (WIN, items), 1)
        for group in range(groups):
            table = maps_ref[group]
            parts = []
            for ref in range(2 * slots):
                block = jnp.maximum(blocks_ref[ref], 0)
                source = jnp.sum(jnp.where(lanes == block, table, 0), axis=1, keepdims=True)
                parts.append((rows == source).astype(jnp.float32))
            onehot = jnp.concatenate(parts, axis=0).astype(jnp.bfloat16)
            picked[group] = jnp.dot(
                onehot, spectra_ref[group], preferred_element_type=jnp.float32
            ).astype(jnp.bfloat16)

    factor = jnp.where(blocks_ref[2 * s] >= 0, scale, 0.0).astype(jnp.float32)
    left = pl.ds(pl.multiple_of(s * 2 * WIN, 2 * WIN), WIN)
    right = pl.ds(pl.multiple_of(s * 2 * WIN + WIN, WIN), WIN)
    for f in range(bins):
        real = slice(f * channels, (f + 1) * channels)
        imag = slice((bins + f) * channels, (bins + f + 1) * channels)
        x_re = [picked[g, left, real] for g in range(groups)]
        x_im = [picked[g, left, imag] for g in range(groups)]
        y_re = jnp.concatenate([picked[g, right, real] for g in range(groups)], axis=0)
        y_im = jnp.concatenate([picked[g, right, imag] for g in range(groups)], axis=0)
        lhs = jnp.concatenate(x_re + x_im, axis=0)
        rhs = jnp.concatenate(
            [
                jnp.concatenate([y_re, -y_im], axis=1),
                jnp.concatenate([y_im, y_re], axis=1),
            ],
            axis=0,
        )
        both = lax.dot_general(lhs, rhs, (((0,), (0,)), ((), ())), preferred_element_type=jnp.float32)
        out_ref[0, f, 0] = both[:, :channels] * factor
        out_ref[0, f, 1] = both[:, channels:] * factor


def stack_pairs(blocks, maps, spectra, slots, channels):
    groups, items, width = spectra.shape
    bins = width // (2 * channels)
    scale = 1.0 / math.sqrt(WIN * groups)
    return pl.pallas_call(
        functools.partial(stack_kernel, groups, slots, bins, channels, scale),
        out_shape=jax.ShapeDtypeStruct((slots, bins, 2, channels, channels), jnp.float32),
        grid_spec=pltpu.PrefetchScalarGridSpec(
            num_scalar_prefetch=1,
            grid=(slots,),
            in_specs=[
                pl.BlockSpec((groups, WIN, NB), lambda s, b: (0, 0, 0)),
                pl.BlockSpec((groups, items, width), lambda s, b: (0, 0, 0), pipeline_mode=pl.Buffered(1)),
            ],
            out_specs=pl.BlockSpec((1, bins, 2, channels, channels), lambda s, b: (s, 0, 0, 0, 0)),
            scratch_shapes=[pltpu.VMEM((groups, 2 * slots * WIN, width), jnp.bfloat16)],
        ),
        compiler_params=pltpu.CompilerParams(
            dimension_semantics=("arbitrary",), vmem_limit_bytes=40 << 20
        ),
        name="stack_pairs",
    )(blocks, maps, spectra)


def per_device(groups, pairs, records, source_map, pair_blocks):
    table = transform_table(records.shape[3])
    local_spec = whiten_spectra(records[0], table)
    items, _, channels = local_spec.shape
    bins = BINS // groups
    own = local_spec.reshape(items, 2, groups, bins, channels)
    own = own.transpose(2, 0, 1, 3, 4).reshape(groups, items, 2 * bins * channels)
    gathered, maps = exchange(own, source_map.reshape(1, WIN, NB), groups, pairs)
    spectra = gathered.reshape(groups, pairs * items, 2 * bins * channels)
    slots = pair_blocks.shape[1]
    return stack_pairs(pair_blocks.reshape(-1), maps, spectra, slots, channels)


def solution(mesh):
    groups, pairs = mesh.shape["tm"], mesh.shape["pairs"]
    return jax.shard_map(
        functools.partial(per_device, groups, pairs),
        mesh=mesh,
        in_specs=(P("tm", "pairs", None, None), P("tm", None), P("pairs", None, None)),
        out_specs=P("pairs", "tm", None, None, None),
        check_vma=False,
    )
```

time: 276 us -> 55.3 us (0.20)
  waiting for transfers between devices: 194 us -> 0 us
  Pallas kernels: 0 us -> 38.1 us
  local copies, waits for them, and re-layouts: 35.6 us -> 5.79 us
  between operations: 13.6 us -> 0.05 us
  matrix products: 19.3 us -> 8.57 us
  other arithmetic: 12.7 us -> 2.45 us
    unnamed x3 -> x0, waiting for transfers between devices: 143 us -> none
    all_gather x1 -> x0, waiting for transfers between devices: 51.1 us -> none  [per_device(): piece = lax.all_gather(local_spec, 'pairs', axis=0, tiled=True)]
    pallas_call x0 -> x2, Pallas kernels: none -> 38.1 us  [the longest x1 32.3 us: exchange(): pl.pallas_call(functools.partial(exchange_kernel, groups, pairs), out_sha...]
    unnamed x9 -> x6, local copies, waits for them, and re-layouts: 29.7 us -> 4.17 us
    dot_general x5 -> x0, matrix products: 10.8 us -> none  [the longest x1 3.95 us: per_device(): jnp.einsum('nr,rkc->nkc', onehot, piece, preferred_element_type=jnp.float32)]
    another operation x2 -> x1, other arithmetic: 10.2 us -> 0.61 us  [the longest x1 9.6 us: cross_stack(): return jnp.stack([real_sum, imag_sum], axis=2)]
    mul x1 -> x0, local copies, waits for them, and re-layouts: 3.14 us -> none  [per_device(): return summed * (valid * norm_factor)[:, None, None, None, None]]
  transfers between devices with their start and end apart: 2 -> 0, of which waited for: 2 -> 0; matrix products, arithmetic and copies ran while one was open for 1% -> 0% of each run, Pallas kernels for 0% -> 0%
where the time goes in v1:
time: 55.3 us; the launch traced here: 55 us
  Pallas kernels  38.1 us (69%)
  matrix products  8.57 us (15%)
  local copies, waits for them, and re-layouts  5.79 us (10%)
  other arithmetic  2.45 us (4%)
    pallas_call x1, Pallas kernels, exchange(): pl.pallas_call(functools.partial(exchange_kernel, groups, pairs), out_sha...  32.3 us
    dot_general x1, matrix products, whiten_spectra(): jnp.einsum('scn,nk->skc', windows, table, preferred_element_type=jnp.floa...  8.57 us
    pallas_call x1, Pallas kernels, stack_pairs(): pl.pallas_call(functools.partial(stack_kernel, groups, slots, bins, chann...  5.86 us
    unnamed x6, local copies, waits for them, and re-layouts  4.17 us
    unnamed x1, other arithmetic  1.34 us

profile of v1, /device:TPU:0, one launch (start us, length us, event | category | flops | bytes accessed | tf_op | source)
XLA Modules:
  0.0 55.0 jit_solution(7527135465958468558)
XLA Ops:
  0.0 0.5 broadcast.69
  0.5 1.3 %reduce.3 = s32[512]{0:T(512)S(1)} reduce(s32[1,512]{1,0:T(1,128)} %param.4, s32[]{:T(128)} %broadcast.69), dimensions={0}, to_apply=%param.4.reduce_sub_computation.3 | reduce | bytes 4100 | tf_op args[1]
  1.9 0.8 %copy.6 = s32[1,6,2]{2,1,0:T(8,128)S(1)} copy(s32[1,6,2]{1,2,0:T(2,128)} %param.5) | data formatting | bytes 96 | tf_op args[2]
  2.6 0.1 reshape.50.blocks_ref
  2.7 0.7 %reshape.53.map_ref = s32[1,16,32]{2,1,0:T(8,128)} reshape(s32[512]{0:T(512)S(1)} %reduce.3) | data formatting | bytes 4096 | tf_op jit(solution)/shard_map/reshape | solution.py:293
  3.4 0.1 subtract_multiply_fusion
  3.4 0.6 %multiply_convert_fusion.2 = (bf16[2048,16]{0,1:T(8,128)(2,1)S(1)}, bf16[2048,16]{0,1:T(8,128)(2,1)S(1)}) fusion(f32[2048]{0:T(1024)S(1)} %subtract_multiply_fusion, s32[16]{0:T(128)S(1)} %iota_add_fusion), kind=kLoop, calls=%fused_computation.19 | loop fusion | flops 622592 | bytes 139328 | tf_op jit(solution)/shard_map/convert
  4.0 8.6 %fusion.2 = f32[32,32,128]{2,1,0:T(8,128)S(1)} fusion(bf16[1,32,128,2048]{3,2,1,0:T(8,128)(2,1)} %param.3, bf16[2048,16]{0,1:T(8,128)(2,1)S(1)} %get-tuple-element.10, bf16[2048,16]{0,1:T(8,128)(2,1)S(1)} %get-tuple-element.9), kind=kOutput, calls=%fused_computation.2 | convolution fusion | flops 537133056 | bytes 17432576 | tf_op jit(solution)/shard_map/scn,nk->skc/dot_general | solution.py:32
  12.6 0.2 fusion.6
  12.8 0.1 maximum_bitcast_fusion.2
  12.9 0.2 multiply_convert_fusion
  13.1 0.8 %reshape.52.own_ref = bf16[2,32,2048]{2,1,0:T(8,128)(2,1)} reshape(bf16[2,32,2,8,128]{4,3,2,1,0:T(8,128)(2,1)S(1)} %bitcast.23) | data formatting | bytes 524288 | tf_op jit(solution)/shard_map/reshape | solution.py:292
  13.9 32.3 %exchange.1 = (bf16[2,16,32,2048]{3,2,1,0:T(8,128)(2,1)}, s32[2,16,32]{2,1,0:T(8,128)}) custom-call(bf16[2,32,2048]{2,1,0:T(8,128)(2,1)} %reshape.52.own_ref, s32[1,16,32]{2,1,0:T(8,128)} %reshape.53.map_ref), custom_call_target="tpu_custom_call" | custom-call | tf_op jit(solution)/shard_map/exchange/pallas_call | solution.py:198
  46.2 0.0 copy-start
  46.2 2.2 %copy-done = bf16[2,16,32,2048]{3,2,1,0:T(8,128)(2,1)S(1)} copy-done((bf16[2,16,32,2048]{3,2,1,0:T(8,128)(2,1)S(1)}, bf16[2,16,32,2048]{3,2,1,0:T(8,128)(2,1)}, u32[]{:S(2)}) %copy-start) | copy-done | bytes 4194328
  48.4 0.0 copy-start.1
  48.4 0.7 %copy-done.1 = s32[2,16,32]{2,1,0:T(8,128)S(1)} copy-done((s32[2,16,32]{2,1,0:T(8,128)S(1)}, s32[2,16,32]{2,1,0:T(8,128)}, u32[]{:S(2)}) %copy-start.1) | copy-done | bytes 4120
  49.1 5.9 %stack_pairs.1 = f32[6,8,2,128,128]{4,3,2,1,0:T(8,128)} custom-call(s32[12]{0:T(128)S(1)} %reshape.50.blocks_ref, s32[2,16,32]{2,1,0:T(8,128)S(1)} %copy-done.1, bf16[2,512,2048]{2,1,0:T(8,128)(2,1)S(1)} %bitcast.21), custom_call_target="tpu_custom_call" | custom-call | tf_op jit(solution)/shard_map/stack_pairs/pallas_call | solution.py:266
  (3 shorter events, 0.1 us)
Async XLA Ops:
  46.2 2.2 %copy-start = (bf16[2,16,32,2048]{3,2,1,0:T(8,128)(2,1)S(1)}, bf16[2,16,32,2048]{3,2,1,0:T(8,128)(2,1)}, u32[]{:S(2)}) copy-start(bf16[2,16,32,2048]{3,2,1,0:T(8,128)(2,1)} %get-tuple-element.8) | copy-start | bytes 12582916
  48.4 0.7 %copy-start.1 = (s32[2,16,32]{2,1,0:T(8,128)S(1)}, s32[2,16,32]{2,1,0:T(8,128)}, u32[]{:S(2)}) copy-start(s32[2,16,32]{2,1,0:T(8,128)} %get-tuple-element.7.maps_ref) | copy-start | bytes 12292

commit v2 on v1

v2 whole, which is shorter than its diff:
```python
import functools
import math

import jax
import jax.numpy as jnp
import numpy as np
from jax import lax
from jax.experimental import pallas as pl
from jax.experimental.pallas import tpu as pltpu
from jax.sharding import PartitionSpec as P

NB = 32
BINS = 16
FIRST_BIN = 64
WIN = 16
MESH = pl.DeviceIdType.MESH


def transform_table(length):
    samples = jnp.arange(length, dtype=jnp.int32)
    bin_index = FIRST_BIN + jnp.arange(BINS, dtype=jnp.int32)
    phases = samples[:, None] * bin_index[None, :] % length
    angles = 2.0 * math.pi / length * phases.astype(jnp.float32)
    taper = 0.5 - 0.5 * jnp.cos(2.0 * math.pi / length * samples.astype(jnp.float32))
    weight_col = (taper / math.sqrt(length))[:, None]
    return jnp.concatenate(
        [jnp.cos(angles) * weight_col, -jnp.sin(angles) * weight_col], axis=1
    ).astype(jnp.bfloat16)


def gather_kernel(groups, pairs, blocks_ref, map_ref, table_ref, records_ref, picked_ref,
                  stream, raw, own, spectra, maps, onehot,
                  load_sems, send_sems, recv_sems, tm_send, map_send, map_recv, keep_sems):
    items, channels, _ = records_ref.shape
    pieces, rows, width = own.shape[1:]
    batch = stream.shape[1]
    bins = width // (2 * channels)
    slots = blocks_ref.shape[1]
    depth = pairs // 4
    layer = 4 * items
    t = lax.axis_index("tm")
    me = lax.axis_index("pairs")
    z = me // 4
    x = (me // 2) % 2
    c = me % 2

    def slot(zz, xx, cc):
        return zz * 4 + xx * 2 + cc

    up, down = me + 4, me - 4
    side = slot(z, 1 - x, c)
    twin = slot(z, x, 1 - c)
    has_up = z < depth - 1
    has_down = z > 0
    batches = items // batch
    depth_in = stream.shape[0]

    def load(i):
        return pltpu.make_async_copy(
            records_ref.at[pl.ds(i * batch, batch)], stream.at[i % depth_in], load_sems.at[i % depth_in]
        )

    for i in range(min(depth_in, batches)):
        load(i).start()

    barrier = pltpu.get_barrier_semaphore()
    for d in range(1, groups):
        pl.semaphore_signal(barrier, inc=1, device_id=((t + d) % groups, me), device_id_type=MESH)
    for other in (side, twin):
        pl.semaphore_signal(barrier, inc=1, device_id=(t, other), device_id_type=MESH)

    @pl.when(has_up)
    def _():
        pl.semaphore_signal(barrier, inc=1, device_id=(t, up), device_id_type=MESH)

    @pl.when(has_down)
    def _():
        pl.semaphore_signal(barrier, inc=1, device_id=(t, down), device_id_type=MESH)

    def send(way, group, place, target, source=None):
        piece = spectra.at[group, place]
        return pltpu.make_async_remote_copy(
            src_ref=piece if source is None else source,
            dst_ref=piece,
            send_sem=send_sems.at[way, group, place],
            recv_sem=recv_sems.at[group, place],
            device_id=(t, target),
            device_id_type=MESH,
        )

    def arrived(group, place):
        pltpu.make_async_copy(
            spectra.at[group, place], spectra.at[group, place], recv_sems.at[group, place]
        ).wait()

    def tm_copy(d, k):
        peer = (t + d) % groups
        place = me * pieces + k
        return pltpu.make_async_remote_copy(
            src_ref=own.at[peer, k],
            dst_ref=spectra.at[t, place],
            send_sem=tm_send.at[d, k],
            recv_sem=recv_sems.at[t, place],
            device_id=(peer, me),
            device_id_type=MESH,
        )

    def map_copy(d):
        peer = (t + d) % groups
        return pltpu.make_async_remote_copy(
            src_ref=map_ref,
            dst_ref=maps.at[t],
            send_sem=map_send.at[d],
            recv_sem=map_recv.at[t],
            device_id=(peer, me),
            device_id_type=MESH,
        )

    def keep(k):
        return pltpu.make_async_copy(own.at[t, k], spectra.at[t, me * pieces + k], keep_sems.at[k])

    def spread(group, place, source, upward, downward):
        if upward is not None:
            @pl.when(upward)
            def _():
                send(0, group, place, up, source).start()
        if downward is not None:
            @pl.when(downward)
            def _():
                send(1, group, place, down, source).start()
        send(2, group, place, side, source).start()
        send(3, group, place, twin, source).start()

    order = [(t + d) % groups for d in range(groups)]

    for k in range(pieces):
        for j in range(rows // batch):
            i = k * (rows // batch) + j
            load(i).wait()
            block = stream[i % depth_in].reshape(batch * channels, records_ref.shape[2])
            both = lax.dot_general(
                table_ref[...], block, (((1,), (1,)), ((), ())), preferred_element_type=jnp.float32
            )
            if i + depth_in < batches:
                load(i + depth_in).start()
            for r in range(batch):
                real = both[:BINS, r * channels:(r + 1) * channels]
                imag = both[BINS:, r * channels:(r + 1) * channels]
                power = jnp.mean(real * real + imag * imag, axis=1, keepdims=True)
                inverse = 1.0 / jnp.sqrt(power + 1e-06)
                raw[j * batch + r, :BINS] = real * inverse
                raw[j * batch + r, BINS:] = imag * inverse
        turned = jnp.transpose(raw[...], (1, 0, 2)).astype(jnp.bfloat16)
        for h in range(groups):
            for part in range(2):
                for f in range(bins):
                    col = (part * bins + f) * channels
                    own[h, k, :, col:col + channels] = turned[part * BINS + h * bins + f]
        if k == 0:
            pl.semaphore_wait(
                barrier, groups + 1 + has_up.astype(jnp.int32) + has_down.astype(jnp.int32)
            )
            for d in range(1, groups):
                map_copy(d).start()
        spread(t, me * pieces + k, own.at[t, k], has_up, has_down)
        for d in range(1, groups):
            tm_copy(d, k).start()
        keep(k).start()

    maps[t] = map_ref[...]
    for k in range(pieces):
        for group in order[1:]:
            arrived(group, me * pieces + k)
            spread(group, me * pieces + k, None, has_up, has_down)

    total = maps.shape[2]
    wanted_lane = lax.broadcasted_iota(jnp.int32, (WIN, total), 0) * NB
    lane = lax.broadcasted_iota(jnp.int32, (WIN, total), 1)
    column = lax.broadcasted_iota(jnp.int32, (WIN, layer), 1)
    for d, group in enumerate(order):
        if d:
            pltpu.make_async_copy(maps.at[group], maps.at[group], map_recv.at[group]).wait()
        table = jnp.broadcast_to(maps[group], (WIN, total))
        for ref in range(2 * slots):
            block = jnp.maximum(blocks_ref[0, ref // 2, ref % 2], 0)
            source = jnp.sum(
                jnp.where(lane == wanted_lane + block, table, 0), axis=1, keepdims=True
            )
            for zz in range(depth):
                hit = (column + zz * layer == source).astype(jnp.float32).astype(jnp.bfloat16)
                onehot[group, zz, ref * WIN:(ref + 1) * WIN, :] = hit
    picked_ref[...] = jnp.zeros_like(picked_ref)
    for k in range(pieces):
        keep(k).wait()

    def pick(zz):
        for group in order:
            for xx in range(2):
                for k in range(pieces):
                    arrived(group, slot(zz, xx, 1 - c) * pieces + k)

        @pl.loop(0, groups)
        def _(group):
            rows_in = spectra[group, pl.ds(zz * 4 * pieces, 4 * pieces)].reshape(layer, width)
            found = jnp.dot(onehot[group, zz], rows_in, preferred_element_type=jnp.float32)
            picked_ref[group] += found.astype(jnp.bfloat16)

    @pl.loop(1, depth + 2)
    def _(step):
        for k in range(pieces):
            for group in order:
                @pl.when(z - step >= 0)
                def _():
                    place = slot(z - step, x, c) * pieces + k
                    arrived(group, place)
                    spread(group, place, None, has_up, None)

                @pl.when(z + step < depth)
                def _():
                    place = slot(z + step, x, c) * pieces + k
                    arrived(group, place)
                    spread(group, place, None, None, has_down)

        for k in range(pieces):
            for group in order:
                for sign in (1, -1):
                    where = z + sign * (step - 1)
                    there = (where >= 0) & (where < depth)

                    @pl.when(there if sign == 1 else there & (step > 1))
                    def _():
                        place = slot(where, 1 - x, c) * pieces + k
                        arrived(group, place)
                        send(3, group, place, twin).start()

        for sign in (1, -1):
            where = z + sign * (step - 2)
            there = (where >= 0) & (where < depth)

            @pl.when(there & (step > (1 if sign == 1 else 2)))
            def _():
                pick(where)

    for d in range(1, groups):
        map_copy(d).wait_send()
        for k in range(pieces):
            tm_copy(d, k).wait_send()

    @pl.loop(0, depth)
    def _(zz):
        for k in range(pieces):
            for group in order:
                place = slot(zz, x, c) * pieces + k

                @pl.when(has_up & (zz <= z))
                def _():
                    send(0, group, place, up).wait_send()

                @pl.when(has_down & (zz >= z))
                def _():
                    send(1, group, place, down).wait_send()

                send(2, group, place, side).wait_send()
                send(3, group, place, twin).wait_send()
                send(3, group, slot(zz, 1 - x, c) * pieces + k, twin).wait_send()


def gather_picked(pair_blocks, source_map, table, records, groups, pairs):
    items, channels, length = records.shape
    slots = pair_blocks.shape[1]
    width = 2 * (BINS // groups) * channels
    rows = min(16, items)
    pieces = items // rows
    batch = min(4, rows)
    dtype = jnp.bfloat16
    vmem = pl.BlockSpec(memory_space=pltpu.VMEM)
    return pl.pallas_call(
        functools.partial(gather_kernel, groups, pairs),
        out_shape=jax.ShapeDtypeStruct((groups, 2 * slots * WIN, width), dtype),
        in_specs=[
            pl.BlockSpec(memory_space=pltpu.SMEM),
            vmem,
            vmem,
            pl.BlockSpec(memory_space=pl.ANY),
        ],
        out_specs=vmem,
        scratch_shapes=[
            pltpu.VMEM((3, batch, channels, length), dtype),
            pltpu.VMEM((rows, 2 * BINS, channels), jnp.float32),
            pltpu.VMEM((groups, pieces, rows, width), dtype),
            pltpu.VMEM((groups, pairs * pieces, rows, width), dtype),
            pltpu.VMEM((groups,) + source_map.shape, jnp.int32),
            pltpu.VMEM((groups, pairs // 4, 2 * slots * WIN, 4 * items), dtype),
            pltpu.SemaphoreType.DMA((3,)),
            pltpu.SemaphoreType.DMA((4, groups, pairs * pieces)),
            pltpu.SemaphoreType.DMA((groups, pairs * pieces)),
            pltpu.SemaphoreType.DMA((groups, pieces)),
            pltpu.SemaphoreType.DMA((groups,)),
            pltpu.SemaphoreType.DMA((groups,)),
            pltpu.SemaphoreType.DMA((pieces,)),
        ],
        compiler_params=pltpu.CompilerParams(
            collective_id=0, has_side_effects=True, vmem_limit_bytes=40 << 20
        ),
        name="gather_picked",
    )(pair_blocks, source_map, table, records)


def stack_kernel(groups, bins, channels, scale, blocks_ref, picked_ref, out_ref):
    s = pl.program_id(0)
    factor = jnp.where(blocks_ref[0, s, 0] >= 0, scale, 0.0).astype(jnp.float32)
    for f in range(bins):
        real = slice(f * channels, (f + 1) * channels)
        imag = slice((bins + f) * channels, (bins + f + 1) * channels)
        x_re = [picked_ref[g, :WIN, real] for g in range(groups)]
        x_im = [picked_ref[g, :WIN, imag] for g in range(groups)]
        y_re = jnp.concatenate([picked_ref[g, WIN:, real] for g in range(groups)], axis=0)
        y_im = jnp.concatenate([picked_ref[g, WIN:, imag] for g in range(groups)], axis=0)
        lhs = jnp.concatenate(x_re + x_im, axis=0)
        rhs = jnp.concatenate(
            [
                jnp.concatenate([y_re, -y_im], axis=1),
                jnp.concatenate([y_im, y_re], axis=1),
            ],
            axis=0,
        )
        both = lax.dot_general(lhs, rhs, (((0,), (0,)), ((), ())), preferred_element_type=jnp.float32)
        out_ref[0, f, 0] = both[:, :channels] * factor
        out_ref[0, f, 1] = both[:, channels:] * factor


def stack_pairs(pair_blocks, picked, channels):
    groups, _, width = picked.shape
    slots = pair_blocks.shape[1]
    bins = width // (2 * channels)
    scale = 1.0 / math.sqrt(WIN * groups)
    return pl.pallas_call(
        functools.partial(stack_kernel, groups, bins, channels, scale),
        out_shape=jax.ShapeDtypeStruct((slots, bins, 2, channels, channels), jnp.float32),
        grid=(slots,),
        in_specs=[
            pl.BlockSpec(memory_space=pltpu.SMEM),
            pl.BlockSpec((groups, 2 * WIN, width), lambda s: (0, s, 0)),
        ],
        out_specs=pl.BlockSpec((1, bins, 2, channels, channels), lambda s: (s, 0, 0, 0, 0)),
        compiler_params=pltpu.CompilerParams(
            dimension_semantics=("arbitrary",), vmem_limit_bytes=40 << 20
        ),
        name="stack_pairs",
    )(pair_blocks, picked)


def per_device(groups, pairs, records, source_map, pair_blocks):
    table = transform_table(records.shape[3]).T
    picked = gather_picked(pair_blocks, source_map, table, records[0], groups, pairs)
    return stack_pairs(pair_blocks, picked, records.shape[2])


def solution(mesh):
    groups, pairs = mesh.shape["tm"], mesh.shape["pairs"]
    return jax.shard_map(
        functools.partial(per_device, groups, pairs),
        mesh=mesh,
        in_specs=(P("tm", "pairs", None, None), P("tm", None), P("pairs", None, None)),
        out_specs=P("pairs", "tm", None, None, None),
        check_vma=False,
    )
```

time: 55.3 us -> 46.3 us (0.84)
  matrix products: 8.57 us -> 0 us
  Pallas kernels: 38.1 us -> 43.9 us
  local copies, waits for them, and re-layouts: 5.79 us -> 1.44 us
  other arithmetic: 2.45 us -> 0.68 us
    dot_general x1 -> x0, matrix products: 8.57 us -> none  [whiten_spectra(): jnp.einsum('scn,nk->skc', windows, table, preferred_element_type=jnp.floa...]
    pallas_call x2, Pallas kernels: 38.1 us -> 43.9 us  [the longest x1 39 us: gather_picked(): pl.pallas_call(functools.partial(gather_kernel, groups, pairs), out_shape...]
    unnamed x6 -> x3, local copies, waits for them, and re-layouts: 4.17 us -> 1.44 us
    reshape x4 -> x0, local copies, waits for them, and re-layouts: 1.61 us -> none  [the longest x1 0.82 us: per_device(): own.transpose(2, 0, 1, 3, 4).reshape(groups, items, 2 * bins * channels)]
    unnamed x1 -> x0, other arithmetic: 1.34 us -> none
where the time goes in v2:
time: 46.3 us; the launch traced here: 46.1 us
  Pallas kernels  43.9 us (95%)
  local copies, waits for them, and re-layouts  1.44 us (3%)
  other arithmetic  0.68 us (1%)
    pallas_call x1, Pallas kernels, gather_picked(): pl.pallas_call(functools.partial(gather_kernel, groups, pairs), out_shape...  39 us
    pallas_call x1, Pallas kernels, stack_pairs(): pl.pallas_call(functools.partial(stack_kernel, groups, bins, channels, sc...  4.94 us
    unnamed x3, local copies, waits for them, and re-layouts  1.44 us

profile of v2, /device:TPU:0, one launch (start us, length us, event | category | flops | bytes accessed | tf_op | source)
XLA Modules:
  0.0 46.1 jit_solution(850224723350806611)
XLA Ops:
  0.0 0.8 %copy.5.blocks_ref = s32[1,6,2]{2,1,0:T(8,128)S(1)} copy(s32[1,6,2]{1,2,0:T(2,128)} %param.5) | data formatting | bytes 96 | tf_op args[2]
  0.8 0.1 subtract_multiply_fusion
  0.8 0.6 %multiply_convert_fusion.1 = (bf16[2048,16]{0,1:T(8,128)(2,1)S(1)}, bf16[2048,16]{0,1:T(8,128)(2,1)S(1)}) fusion(f32[2048]{0:T(1024)S(1)} %subtract_multiply_fusion, s32[16]{0:T(128)S(1)} %iota_add_fusion), kind=kLoop, calls=%fused_computation.8 | loop fusion | flops 622592 | bytes 139328 | tf_op jit(solution)/shard_map/convert
  1.5 0.0 copy-start
  1.5 0.7 %copy-done = s32[1,512]{1,0:T(1,128)S(1)} copy-done((s32[1,512]{1,0:T(1,128)S(1)}, s32[1,512]{1,0:T(1,128)}, u32[]{:S(2)}) %copy-start) | copy-done | bytes 2072
  2.1 39.0 %gather_picked.1.picked_ref = bf16[2,192,2048]{2,1,0:T(8,128)(2,1)S(1)} custom-call(s32[1,6,2]{2,1,0:T(8,128)S(1)} %copy.5.blocks_ref, s32[1,512]{1,0:T(1,128)S(1)} %copy-done, bf16[32,2048]{1,0:T(8,128)(2,1)S(1)} %maximum_bitcast_fusion.table_ref, bf16[32,128,2048]{2,1,0:T(8,128)(2,1)} %bitcast.3), custom_call_target="tpu_custom_call" | custom-call | tf_op jit(solution)/shard_map/gather_picked/pallas_call | solution.py:277
  41.2 4.9 %stack_pairs.1 = f32[6,8,2,128,128]{4,3,2,1,0:T(8,128)} custom-call(s32[1,6,2]{2,1,0:T(8,128)S(1)} %copy.5.blocks_ref, bf16[2,192,2048]{2,1,0:T(8,128)(2,1)S(1)} %gather_picked.1.picked_ref), custom_call_target="tpu_custom_call" | custom-call | tf_op jit(solution)/shard_map/stack_pairs/pallas_call | solution.py:337
  (2 shorter events, 0.0 us)
Async XLA Ops:
  1.5 0.7 %copy-start = (s32[1,512]{1,0:T(1,128)S(1)}, s32[1,512]{1,0:T(1,128)}, u32[]{:S(2)}) copy-start(s32[1,512]{1,0:T(1,128)} %map_ref.1) | copy-start | bytes 6148

commit v3 on v2

--- a/solution.py
+++ b/solution.py
@@ -17,20 +17,17 @@
 
 
 def transform_table(length):
-    samples = jnp.arange(length, dtype=jnp.int32)
-    bin_index = FIRST_BIN + jnp.arange(BINS, dtype=jnp.int32)
-    phases = samples[:, None] * bin_index[None, :] % length
-    angles = 2.0 * math.pi / length * phases.astype(jnp.float32)
-    taper = 0.5 - 0.5 * jnp.cos(2.0 * math.pi / length * samples.astype(jnp.float32))
-    weight_col = (taper / math.sqrt(length))[:, None]
-    return jnp.concatenate(
-        [jnp.cos(angles) * weight_col, -jnp.sin(angles) * weight_col], axis=1
-    ).astype(jnp.bfloat16)
+    samples = np.arange(length)
+    phases = samples[None, :] * (FIRST_BIN + np.arange(BINS))[:, None] % length
+    angles = 2.0 * np.pi / length * phases
+    weight = (0.5 - 0.5 * np.cos(2.0 * np.pi / length * samples)) / math.sqrt(length)
+    rows = np.concatenate([np.cos(angles) * weight, -np.sin(angles) * weight])
+    return rows.astype(np.float32).astype(jnp.bfloat16)
 
 
 def gather_kernel(groups, pairs, blocks_ref, map_ref, table_ref, records_ref, picked_ref,
-                  stream, raw, own, spectra, maps, onehot,
-                  load_sems, send_sems, recv_sems, tm_send, map_send, map_recv, keep_sems):
+                  table, stream, raw, own, spectra, maps, onehot,
+                  table_sem, load_sems, send_sems, recv_sems, tm_send, map_send, map_recv, keep_sems):
     items, channels, _ = records_ref.shape
     pieces, rows, width = own.shape[1:]
     batch = stream.shape[1]
@@ -60,6 +57,8 @@
             records_ref.at[pl.ds(i * batch, batch)], stream.at[i % depth_in], load_sems.at[i % depth_in]
         )
 
+    fetch_table = pltpu.make_async_copy(table_ref, table, table_sem.at[0])
+    fetch_table.start()
     for i in range(min(depth_in, batches)):
         load(i).start()
 
@@ -119,30 +118,86 @@
     def keep(k):
         return pltpu.make_async_copy(own.at[t, k], spectra.at[t, me * pieces + k], keep_sems.at[k])
 
-    def spread(group, place, source, upward, downward):
-        if upward is not None:
-            @pl.when(upward)
+    def over_line(where, k):
+        half = k % 2 == 1
+        below = (where == z - 1) & ((where == 0) | ((where == depth - 2) & half))
+        above = (where == z + 1) & ((where == depth - 1) | ((where == 1) & half))
+        return below | above
+
+    def when_sent(condition, way, group, place, target, source=None):
+        @pl.when(condition)
+        def _():
+            send(way, group, place, target, source).start()
+
+    def first_spread(group, k, source=None):
+        place = me * pieces + k
+        send(2, group, place, side, source).start()
+        when_sent(has_up, 0, group, place, up, source)
+        when_sent(has_down, 1, group, place, down, source)
+        send(3, group, place, twin, source).start()
+
+    def column_arrival(step, group, k):
+        for sign, onward, way, target in ((-1, has_up, 0, up), (1, has_down, 1, down)):
+            where = z + sign * step
+
+            @pl.when((where >= 0) & (where < depth))
             def _():
-                send(0, group, place, up, source).start()
-        if downward is not None:
-            @pl.when(downward)
+                place = slot(where, x, c) * pieces + k
+                arrived(group, place)
+                when_sent(onward, way, group, place, target)
+                when_sent(jnp.logical_not(over_line(where, k)), 2, group, place, side)
+                send(3, group, place, twin).start()
+
+    def lift(k):
+        return (z == 0) | ((z == depth - 2) & (k % 2 == 1))
+
+    def lower(k):
+        return (z == depth - 1) | ((z == 1) & (k % 2 == 1))
+
+    def side_arrival(step, group, k):
+        if isinstance(step, int):
+            place = side * pieces + k
+            arrived(group, place)
+            when_sent(lift(k), 0, group, place, up)
+            when_sent(lower(k), 1, group, place, down)
+            send(3, group, place, twin).start()
+            return
+        for sign in (-1, 1):
+            where = z + sign * step
+
+            @pl.when((where >= 0) & (where < depth))
             def _():
-                send(1, group, place, down, source).start()
-        send(2, group, place, side, source).start()
-        send(3, group, place, twin, source).start()
+                place = slot(where, 1 - x, c) * pieces + k
+                arrived(group, place)
+                send(3, group, place, twin).start()
 
     order = [(t + d) % groups for d in range(groups)]
 
+    def early(j):
+        if j == 1:
+            for group in order[1:]:
+                arrived(group, me * pieces)
+                first_spread(group, 0)
+        if j == 2:
+            column_arrival(1, order[0], 0)
+        if j == 3:
+            side_arrival(0, order[0], 0)
+            for group in order[1:]:
+                column_arrival(1, group, 0)
+
+    fetch_table.wait()
     for k in range(pieces):
         for j in range(rows // batch):
             i = k * (rows // batch) + j
             load(i).wait()
             block = stream[i % depth_in].reshape(batch * channels, records_ref.shape[2])
             both = lax.dot_general(
-                table_ref[...], block, (((1,), (1,)), ((), ())), preferred_element_type=jnp.float32
+                table[...], block, (((1,), (1,)), ((), ())), preferred_element_type=jnp.float32
             )
             if i + depth_in < batches:
                 load(i + depth_in).start()
+            if k == 1:
+                early(j)
             for r in range(batch):
                 real = both[:BINS, r * channels:(r + 1) * channels]
                 imag = both[BINS:, r * channels:(r + 1) * channels]
@@ -162,16 +217,24 @@
             )
             for d in range(1, groups):
                 map_copy(d).start()
-        spread(t, me * pieces + k, own.at[t, k], has_up, has_down)
         for d in range(1, groups):
             tm_copy(d, k).start()
+        first_spread(t, k, own.at[t, k])
         keep(k).start()
 
     maps[t] = map_ref[...]
-    for k in range(pieces):
+    split = pieces > 1
+    for k in range(1 if split else 0, pieces):
         for group in order[1:]:
             arrived(group, me * pieces + k)
-            spread(group, me * pieces + k, None, has_up, has_down)
+            first_spread(group, k)
+    for k in range(1 if split else 0, pieces):
+        for group in order:
+            column_arrival(1, group, k)
+    for k in range(pieces):
+        for group in order:
+            if not (split and k == 0) or group is not order[0]:
+                side_arrival(0, group, k)
 
     total = maps.shape[2]
     wanted_lane = lax.broadcasted_iota(jnp.int32, (WIN, total), 0) * NB
@@ -182,7 +245,7 @@
             pltpu.make_async_copy(maps.at[group], maps.at[group], map_recv.at[group]).wait()
         table = jnp.broadcast_to(maps[group], (WIN, total))
         for ref in range(2 * slots):
-            block = jnp.maximum(blocks_ref[0, ref // 2, ref % 2], 0)
+            block = jnp.maximum(blocks_ref[0, ref // 2:ref // 2 + 1, ref % 2:ref % 2 + 1], 0)
             source = jnp.sum(
                 jnp.where(lane == wanted_lane + block, table, 0), axis=1, keepdims=True
             )
@@ -205,33 +268,14 @@
             found = jnp.dot(onehot[group, zz], rows_in, preferred_element_type=jnp.float32)
             picked_ref[group] += found.astype(jnp.bfloat16)
 
-    @pl.loop(1, depth + 2)
+    @pl.loop(2, depth + 2)
     def _(step):
         for k in range(pieces):
             for group in order:
-                @pl.when(z - step >= 0)
-                def _():
-                    place = slot(z - step, x, c) * pieces + k
-                    arrived(group, place)
-                    spread(group, place, None, has_up, None)
-
-                @pl.when(z + step < depth)
-                def _():
-                    place = slot(z + step, x, c) * pieces + k
-                    arrived(group, place)
-                    spread(group, place, None, None, has_down)
-
+                column_arrival(step, group, k)
         for k in range(pieces):
             for group in order:
-                for sign in (1, -1):
-                    where = z + sign * (step - 1)
-                    there = (where >= 0) & (where < depth)
-
-                    @pl.when(there if sign == 1 else there & (step > 1))
-                    def _():
-                        place = slot(where, 1 - x, c) * pieces + k
-                        arrived(group, place)
-                        send(3, group, place, twin).start()
+                side_arrival(step - 1, group, k)
 
         for sign in (1, -1):
             where = z + sign * (step - 2)
@@ -245,6 +289,16 @@
         map_copy(d).wait_send()
         for k in range(pieces):
             tm_copy(d, k).wait_send()
+
+    for k in range(pieces):
+        for group in order:
+            @pl.when(lift(k))
+            def _():
+                send(0, group, side * pieces + k, up).wait_send()
+
+            @pl.when(lower(k))
+            def _():
+                send(1, group, side * pieces + k, down).wait_send()
 
     @pl.loop(0, depth)
     def _(zz):
@@ -260,7 +314,10 @@
                 def _():
                     send(1, group, place, down).wait_send()
 
-                send(2, group, place, side).wait_send()
+                @pl.when(jnp.logical_not(over_line(zz, k)))
+                def _():
+                    send(2, group, place, side).wait_send()
+
                 send(3, group, place, twin).wait_send()
                 send(3, group, slot(zz, 1 - x, c) * pieces + k, twin).wait_send()
 
@@ -278,19 +335,21 @@
         functools.partial(gather_kernel, groups, pairs),
         out_shape=jax.ShapeDtypeStruct((groups, 2 * slots * WIN, width), dtype),
         in_specs=[
-            pl.BlockSpec(memory_space=pltpu.SMEM),
             vmem,
             vmem,
+            pl.BlockSpec(memory_space=pl.ANY),
             pl.BlockSpec(memory_space=pl.ANY),
         ],
         out_specs=vmem,
         scratch_shapes=[
+            pltpu.VMEM((2 * BINS, length), dtype),
             pltpu.VMEM((3, batch, channels, length), dtype),
             pltpu.VMEM((rows, 2 * BINS, channels), jnp.float32),
             pltpu.VMEM((groups, pieces, rows, width), dtype),
             pltpu.VMEM((groups, pairs * pieces, rows, width), dtype),
             pltpu.VMEM((groups,) + source_map.shape, jnp.int32),
             pltpu.VMEM((groups, pairs // 4, 2 * slots * WIN, 4 * items), dtype),
+            pltpu.SemaphoreType.DMA((1,)),
             pltpu.SemaphoreType.DMA((3,)),
             pltpu.SemaphoreType.DMA((4, groups, pairs * pieces)),
             pltpu.SemaphoreType.DMA((groups, pairs * pieces)),
@@ -306,27 +365,41 @@
     )(pair_blocks, source_map, table, records)
 
 
-def stack_kernel(groups, bins, channels, scale, blocks_ref, picked_ref, out_ref):
-    s = pl.program_id(0)
-    factor = jnp.where(blocks_ref[0, s, 0] >= 0, scale, 0.0).astype(jnp.float32)
-    for f in range(bins):
-        real = slice(f * channels, (f + 1) * channels)
-        imag = slice((bins + f) * channels, (bins + f + 1) * channels)
-        x_re = [picked_ref[g, :WIN, real] for g in range(groups)]
-        x_im = [picked_ref[g, :WIN, imag] for g in range(groups)]
-        y_re = jnp.concatenate([picked_ref[g, WIN:, real] for g in range(groups)], axis=0)
-        y_im = jnp.concatenate([picked_ref[g, WIN:, imag] for g in range(groups)], axis=0)
-        lhs = jnp.concatenate(x_re + x_im, axis=0)
-        rhs = jnp.concatenate(
-            [
-                jnp.concatenate([y_re, -y_im], axis=1),
-                jnp.concatenate([y_im, y_re], axis=1),
-            ],
-            axis=0,
-        )
-        both = lax.dot_general(lhs, rhs, (((0,), (0,)), ((), ())), preferred_element_type=jnp.float32)
-        out_ref[0, f, 0] = both[:, :channels] * factor
-        out_ref[0, f, 1] = both[:, channels:] * factor
+def stack_kernel(groups, scale, blocks_ref, picked_ref, out_ref, done, sems):
+    slots, bins, _, channels, _ = out_ref.shape
+
+    def write(s, f):
+        return pltpu.make_async_copy(done.at[s, f], out_ref.at[s, f], sems.at[s, f])
+
+    for s in range(slots):
+        factor = jnp.where(blocks_ref[0, s:s + 1, 0:1] >= 0, scale, 0.0).astype(jnp.float32)
+        factor = jnp.broadcast_to(factor, (channels, channels))
+        left = slice(2 * s * WIN, (2 * s + 1) * WIN)
+        right = slice((2 * s + 1) * WIN, (2 * s + 2) * WIN)
+        for f in range(bins):
+            real = slice(f * channels, (f + 1) * channels)
+            imag = slice((bins + f) * channels, (bins + f + 1) * channels)
+            x_re = [picked_ref[g, left, real] for g in range(groups)]
+            x_im = [picked_ref[g, left, imag] for g in range(groups)]
+            y_re = jnp.concatenate([picked_ref[g, right, real] for g in range(groups)], axis=0)
+            y_im = jnp.concatenate([picked_ref[g, right, imag] for g in range(groups)], axis=0)
+            lhs = jnp.concatenate(x_re + x_im, axis=0)
+            rhs = jnp.concatenate(
+                [
+                    jnp.concatenate([y_re, -y_im], axis=1),
+                    jnp.concatenate([y_im, y_re], axis=1),
+                ],
+                axis=0,
+            )
+            both = lax.dot_general(
+                lhs, rhs, (((0,), (0,)), ((), ())), preferred_element_type=jnp.float32
+            )
+            done[s, f, 0] = both[:, :channels] * factor
+            done[s, f, 1] = both[:, channels:] * factor
+            write(s, f).start()
+    for s in range(slots):
+        for f in range(bins):
+            write(s, f).wait()
 
 
 def stack_pairs(pair_blocks, picked, channels):
@@ -334,24 +407,21 @@
     slots = pair_blocks.shape[1]
     bins = width // (2 * channels)
     scale = 1.0 / math.sqrt(WIN * groups)
+    vmem = pl.BlockSpec(memory_space=pltpu.VMEM)
+    shape = (slots, bins, 2, channels, channels)
     return pl.pallas_call(
-        functools.partial(stack_kernel, groups, bins, channels, scale),
-        out_shape=jax.ShapeDtypeStruct((slots, bins, 2, channels, channels), jnp.float32),
-        grid=(slots,),
-        in_specs=[
-            pl.BlockSpec(memory_space=pltpu.SMEM),
-            pl.BlockSpec((groups, 2 * WIN, width), lambda s: (0, s, 0)),
-        ],
-        out_specs=pl.BlockSpec((1, bins, 2, channels, channels), lambda s: (s, 0, 0, 0, 0)),
-        compiler_params=pltpu.CompilerParams(
-            dimension_semantics=("arbitrary",), vmem_limit_bytes=40 << 20
-        ),
+        functools.partial(stack_kernel, groups, scale),
+        out_shape=jax.ShapeDtypeStruct(shape, jnp.float32),
+        in_specs=[vmem, vmem],
+        out_specs=pl.BlockSpec(memory_space=pl.ANY),
+        scratch_shapes=[pltpu.VMEM(shape, jnp.float32), pltpu.SemaphoreType.DMA((slots, bins))],
+        compiler_params=pltpu.CompilerParams(vmem_limit_bytes=40 << 20),
         name="stack_pairs",
     )(pair_blocks, picked)
 
 
 def per_device(groups, pairs, records, source_map, pair_blocks):
-    table = transform_table(records.shape[3]).T
+    table = jnp.asarray(transform_table(records.shape[3]))
     picked = gather_picked(pair_blocks, source_map, table, records[0], groups, pairs)
     return stack_pairs(pair_blocks, picked, records.shape[2])
 

time: 46.3 us -> 46.1 us (level)
  local copies, waits for them, and re-layouts: 1.44 us -> 2.35 us
  other arithmetic: 0.68 us -> 0 us
    pallas_call x1, Pallas kernels: 4.94 us -> 3.26 us  [stack_pairs(): pl.pallas_call(functools.partial(stack_kernel, groups, scale), out_shape=...]
    pallas_call x1, Pallas kernels: 39 us -> 40.3 us  [gather_picked(): pl.pallas_call(functools.partial(gather_kernel, groups, pairs), out_shape...]
    unnamed x3 -> x5, local copies, waits for them, and re-layouts: 1.44 us -> 2.35 us
    another operation x1 -> x0, other arithmetic: 0.61 us -> none
where the time goes in v3:
time: 46.1 us; the launch traced here: 46 us
  Pallas kernels  43.6 us (95%)
  local copies, waits for them, and re-layouts  2.35 us (5%)
    pallas_call x1, Pallas kernels, gather_picked(): pl.pallas_call(functools.partial(gather_kernel, groups, pairs), out_shape...  40.3 us
    pallas_call x1, Pallas kernels, stack_pairs(): pl.pallas_call(functools.partial(stack_kernel, groups, scale), out_shape=...  3.26 us
    unnamed x5, local copies, waits for them, and re-layouts  2.35 us

profile of v3, /device:TPU:0, one launch (start us, length us, event | category | flops | bytes accessed | tf_op | source)
XLA Modules:
  0.0 46.0 jit_solution(15948586500352293161)
XLA Ops:
  0.0 0.8 %copy.6.blocks_ref = s32[1,6,2]{2,1,0:T(8,128)S(1)} copy(s32[1,6,2]{1,2,0:T(2,128)} %param.6) | data formatting | bytes 96 | tf_op args[2]
  0.8 0.0 copy-start
  0.8 0.9 %copy-done = bf16[32,2048]{1,0:T(8,128)(2,1)S(1)} copy-done((bf16[32,2048]{1,0:T(8,128)(2,1)S(1)}, bf16[32,2048]{1,0:T(8,128)(2,1)}, u32[]{:S(2)}) %copy-start) | copy-done | bytes 131096
  1.7 0.0 copy-start.1
  1.7 0.7 %copy-done.1 = s32[1,512]{1,0:T(1,128)S(1)} copy-done((s32[1,512]{1,0:T(1,128)S(1)}, s32[1,512]{1,0:T(1,128)}, u32[]{:S(2)}) %copy-start.1) | copy-done | bytes 2072
  2.4 40.3 %gather_picked.1.picked_ref = bf16[2,192,2048]{2,1,0:T(8,128)(2,1)S(1)} custom-call(s32[1,6,2]{2,1,0:T(8,128)S(1)} %copy.6.blocks_ref, s32[1,512]{1,0:T(1,128)S(1)} %copy-done.1, bf16[32,2048]{1,0:T(8,128)(2,1)S(1)} %copy-done, bf16[32,128,2048]{2,1,0:T(8,128)(2,1)} %bitcast.1), custom_call_target="tpu_custom_call" | custom-call | tf_op jit(solution)/shard_map/gather_picked/pallas_call | solution.py:334
  42.7 3.3 %stack_pairs.1 = f32[6,8,2,128,128]{4,3,2,1,0:T(8,128)} custom-call(s32[1,6,2]{2,1,0:T(8,128)S(1)} %copy.6.blocks_ref, bf16[2,192,2048]{2,1,0:T(8,128)(2,1)S(1)} %gather_picked.1.picked_ref), custom_call_target="tpu_custom_call" | custom-call | tf_op jit(solution)/shard_map/stack_pairs/pallas_call | solution.py:412
Async XLA Ops:
  0.8 0.9 %copy-start = (bf16[32,2048]{1,0:T(8,128)(2,1)S(1)}, bf16[32,2048]{1,0:T(8,128)(2,1)}, u32[]{:S(2)}) copy-start(bf16[32,2048]{1,0:T(8,128)(2,1)} %constant.2.clone.table_ref) | copy-start | bytes 393220
  1.7 0.7 %copy-start.1 = (s32[1,512]{1,0:T(1,128)S(1)}, s32[1,512]{1,0:T(1,128)}, u32[]{:S(2)}) copy-start(s32[1,512]{1,0:T(1,128)} %map_ref.1) | copy-start | bytes 6148

commit v4 on v3

--- a/solution.py
+++ b/solution.py
@@ -26,13 +26,13 @@
 
 
 def gather_kernel(groups, pairs, blocks_ref, map_ref, table_ref, records_ref, picked_ref,
-                  table, stream, raw, own, spectra, maps, onehot,
-                  table_sem, load_sems, send_sems, recv_sems, tm_send, map_send, map_recv, keep_sems):
+                  table, blocks, stream, raw, own, spectra, maps, onehot,
+                  small_sems, load_sems, send_sems, recv_sems, tm_send, map_send, map_recv, keep_sems):
     items, channels, _ = records_ref.shape
     pieces, rows, width = own.shape[1:]
     batch = stream.shape[1]
     bins = width // (2 * channels)
-    slots = blocks_ref.shape[1]
+    slots = blocks.shape[2]
     depth = pairs // 4
     layer = 4 * items
     t = lax.axis_index("tm")
@@ -57,8 +57,12 @@
             records_ref.at[pl.ds(i * batch, batch)], stream.at[i % depth_in], load_sems.at[i % depth_in]
         )
 
-    fetch_table = pltpu.make_async_copy(table_ref, table, table_sem.at[0])
+    fetch_table = pltpu.make_async_copy(table_ref, table, small_sems.at[0])
     fetch_table.start()
+    fetch_blocks = pltpu.make_async_copy(blocks_ref, blocks, small_sems.at[1])
+    fetch_blocks.start()
+    keep_map = pltpu.make_async_copy(map_ref, maps.at[t], small_sems.at[2])
+    keep_map.start()
     for i in range(min(depth_in, batches)):
         load(i).start()
 
@@ -118,11 +122,8 @@
     def keep(k):
         return pltpu.make_async_copy(own.at[t, k], spectra.at[t, me * pieces + k], keep_sems.at[k])
 
-    def over_line(where, k):
-        half = k % 2 == 1
-        below = (where == z - 1) & ((where == 0) | ((where == depth - 2) & half))
-        above = (where == z + 1) & ((where == depth - 1) | ((where == 1) & half))
-        return below | above
+    def over_line(where):
+        return ((where == z - 1) & (where == 0)) | ((where == z + 1) & (where == depth - 1))
 
     def when_sent(condition, way, group, place, target, source=None):
         @pl.when(condition)
@@ -145,21 +146,18 @@
                 place = slot(where, x, c) * pieces + k
                 arrived(group, place)
                 when_sent(onward, way, group, place, target)
-                when_sent(jnp.logical_not(over_line(where, k)), 2, group, place, side)
+                when_sent(jnp.logical_not(over_line(where)), 2, group, place, side)
                 send(3, group, place, twin).start()
 
-    def lift(k):
-        return (z == 0) | ((z == depth - 2) & (k % 2 == 1))
-
-    def lower(k):
-        return (z == depth - 1) | ((z == 1) & (k % 2 == 1))
+    lift = z == 0
+    lower = z == depth - 1
 
     def side_arrival(step, group, k):
         if isinstance(step, int):
             place = side * pieces + k
             arrived(group, place)
-            when_sent(lift(k), 0, group, place, up)
-            when_sent(lower(k), 1, group, place, down)
+            when_sent(lift, 0, group, place, up)
+            when_sent(lower, 1, group, place, down)
             send(3, group, place, twin).start()
             return
         for sign in (-1, 1):
@@ -222,7 +220,8 @@
         first_spread(t, k, own.at[t, k])
         keep(k).start()
 
-    maps[t] = map_ref[...]
+    fetch_blocks.wait()
+    keep_map.wait()
     split = pieces > 1
     for k in range(1 if split else 0, pieces):
         for group in order[1:]:
@@ -243,12 +242,13 @@
     for d, group in enumerate(order):
         if d:
             pltpu.make_async_copy(maps.at[group], maps.at[group], map_recv.at[group]).wait()
-        table = jnp.broadcast_to(maps[group], (WIN, total))
+        row = jnp.broadcast_to(maps[group], (WIN, total))
         for ref in range(2 * slots):
-            block = jnp.maximum(blocks_ref[0, ref // 2:ref // 2 + 1, ref % 2:ref % 2 + 1], 0)
+            block = blocks[0, ref % 2:ref % 2 + 1, ref // 2:ref // 2 + 1]
             source = jnp.sum(
-                jnp.where(lane == wanted_lane + block, table, 0), axis=1, keepdims=True
+                jnp.where(lane == wanted_lane + block, row, 0), axis=1, keepdims=True
             )
+            source = jnp.where(block >= 0, source, -1)
             for zz in range(depth):
                 hit = (column + zz * layer == source).astype(jnp.float32).astype(jnp.bfloat16)
                 onehot[group, zz, ref * WIN:(ref + 1) * WIN, :] = hit
@@ -292,11 +292,11 @@
 
     for k in range(pieces):
         for group in order:
-            @pl.when(lift(k))
+            @pl.when(lift)
             def _():
                 send(0, group, side * pieces + k, up).wait_send()
 
-            @pl.when(lower(k))
+            @pl.when(lower)
             def _():
                 send(1, group, side * pieces + k, down).wait_send()
 
@@ -314,7 +314,7 @@
                 def _():
                     send(1, group, place, down).wait_send()
 
-                @pl.when(jnp.logical_not(over_line(zz, k)))
+                @pl.when(jnp.logical_not(over_line(zz)))
                 def _():
                     send(2, group, place, side).wait_send()
 
@@ -324,7 +324,7 @@
 
 def gather_picked(pair_blocks, source_map, table, records, groups, pairs):
     items, channels, length = records.shape
-    slots = pair_blocks.shape[1]
+    slots = pair_blocks.shape[2]
     width = 2 * (BINS // groups) * channels
     rows = min(16, items)
     pieces = items // rows
@@ -334,22 +334,18 @@
     return pl.pallas_call(
         functools.partial(gather_kernel, groups, pairs),
         out_shape=jax.ShapeDtypeStruct((groups, 2 * slots * WIN, width), dtype),
-        in_specs=[
-            vmem,
-            vmem,
-            pl.BlockSpec(memory_space=pl.ANY),
-            pl.BlockSpec(memory_space=pl.ANY),
-        ],
+        in_specs=[pl.BlockSpec(memory_space=pltpu.HBM)] * 4,
         out_specs=vmem,
         scratch_shapes=[
             pltpu.VMEM((2 * BINS, length), dtype),
+            pltpu.VMEM(pair_blocks.shape, jnp.int32),
             pltpu.VMEM((3, batch, channels, length), dtype),
             pltpu.VMEM((rows, 2 * BINS, channels), jnp.float32),
             pltpu.VMEM((groups, pieces, rows, width), dtype),
             pltpu.VMEM((groups, pairs * pieces, rows, width), dtype),
             pltpu.VMEM((groups,) + source_map.shape, jnp.int32),
             pltpu.VMEM((groups, pairs // 4, 2 * slots * WIN, 4 * items), dtype),
-            pltpu.SemaphoreType.DMA((1,)),
+            pltpu.SemaphoreType.DMA((3,)),
             pltpu.SemaphoreType.DMA((3,)),
             pltpu.SemaphoreType.DMA((4, groups, pairs * pieces)),
             pltpu.SemaphoreType.DMA((groups, pairs * pieces)),
@@ -359,21 +355,19 @@
             pltpu.SemaphoreType.DMA((pieces,)),
         ],
         compiler_params=pltpu.CompilerParams(
-            collective_id=0, has_side_effects=True, vmem_limit_bytes=40 << 20
+            collective_id=0, has_side_effects=True, vmem_limit_bytes=63 << 20
         ),
         name="gather_picked",
     )(pair_blocks, source_map, table, records)
 
 
-def stack_kernel(groups, scale, blocks_ref, picked_ref, out_ref, done, sems):
+def stack_kernel(groups, scale, picked_ref, out_ref, done, sems):
     slots, bins, _, channels, _ = out_ref.shape
 
     def write(s, f):
         return pltpu.make_async_copy(done.at[s, f], out_ref.at[s, f], sems.at[s, f])
 
     for s in range(slots):
-        factor = jnp.where(blocks_ref[0, s:s + 1, 0:1] >= 0, scale, 0.0).astype(jnp.float32)
-        factor = jnp.broadcast_to(factor, (channels, channels))
         left = slice(2 * s * WIN, (2 * s + 1) * WIN)
         right = slice((2 * s + 1) * WIN, (2 * s + 2) * WIN)
         for f in range(bins):
@@ -394,17 +388,16 @@
             both = lax.dot_general(
                 lhs, rhs, (((0,), (0,)), ((), ())), preferred_element_type=jnp.float32
             )
-            done[s, f, 0] = both[:, :channels] * factor
-            done[s, f, 1] = both[:, channels:] * factor
+            done[s, f, 0] = both[:, :channels] * scale
+            done[s, f, 1] = both[:, channels:] * scale
             write(s, f).start()
     for s in range(slots):
         for f in range(bins):
             write(s, f).wait()
 
 
-def stack_pairs(pair_blocks, picked, channels):
+def stack_pairs(slots, picked, channels):
     groups, _, width = picked.shape
-    slots = pair_blocks.shape[1]
     bins = width // (2 * channels)
     scale = 1.0 / math.sqrt(WIN * groups)
     vmem = pl.BlockSpec(memory_space=pltpu.VMEM)
@@ -412,18 +405,19 @@
     return pl.pallas_call(
         functools.partial(stack_kernel, groups, scale),
         out_shape=jax.ShapeDtypeStruct(shape, jnp.float32),
-        in_specs=[vmem, vmem],
+        in_specs=[vmem],
         out_specs=pl.BlockSpec(memory_space=pl.ANY),
         scratch_shapes=[pltpu.VMEM(shape, jnp.float32), pltpu.SemaphoreType.DMA((slots, bins))],
         compiler_params=pltpu.CompilerParams(vmem_limit_bytes=40 << 20),
         name="stack_pairs",
-    )(pair_blocks, picked)
+    )(picked)
 
 
 def per_device(groups, pairs, records, source_map, pair_blocks):
     table = jnp.asarray(transform_table(records.shape[3]))
-    picked = gather_picked(pair_blocks, source_map, table, records[0], groups, pairs)
-    return stack_pairs(pair_blocks, picked, records.shape[2])
+    blocks = pair_blocks.transpose(0, 2, 1)
+    picked = gather_picked(blocks, source_map, table, records[0], groups, pairs)
+    return stack_pairs(pair_blocks.shape[1], picked, records.shape[2])
 
 
 def solution(mesh):

time: 46.1 us -> 46.6 us (1.011)
  Pallas kernels: 43.6 us -> 45 us
  local copies, waits for them, and re-layouts: 2.35 us -> 1.4 us
    pallas_call x1, Pallas kernels: 40.3 us -> 41.8 us  [gather_picked(): pl.pallas_call(functools.partial(gather_kernel, groups, pairs), out_shape...]
    unnamed x5 -> x2, local copies, waits for them, and re-layouts: 2.35 us -> 1.4 us
where the time goes in v4:
time: 46.6 us; the launch traced here: 46.4 us
  Pallas kernels  45 us (97%)
  local copies, waits for them, and re-layouts  1.4 us (3%)
    pallas_call x1, Pallas kernels, gather_picked(): pl.pallas_call(functools.partial(gather_kernel, groups, pairs), out_shape...  41.8 us
    pallas_call x1, Pallas kernels, stack_pairs(): pl.pallas_call(functools.partial(stack_kernel, groups, scale), out_shape=...  3.26 us
    unnamed x2, local copies, waits for them, and re-layouts  1.4 us

profile of v4, /device:TPU:0, one launch (start us, length us, event | category | flops | bytes accessed | tf_op | source)
XLA Modules:
  0.0 46.4 jit_solution(4191015637920579588)
XLA Ops:
  0.0 41.8 %gather_picked.1.picked_ref = bf16[2,192,2048]{2,1,0:T(8,128)(2,1)} custom-call(s32[1,2,6]{2,1,0:T(2,128)} %bitcast.3, s32[1,512]{1,0:T(1,128)} %map_ref.1, bf16[32,2048]{1,0:T(8,128)(2,1)} %constant.2.clone.table_ref, bf16[32,128,2048]{2,1,0:T(8,128)(2,1)} %bitcast.2), custom_call_target="tpu_custom_call" | custom-call | tf_op jit(solution)/shard_map/gather_picked/pallas_call | solution.py:334
  41.8 0.0 copy-start
  41.8 1.4 %copy-done = bf16[2,192,2048]{2,1,0:T(8,128)(2,1)S(1)} copy-done((bf16[2,192,2048]{2,1,0:T(8,128)(2,1)S(1)}, bf16[2,192,2048]{2,1,0:T(8,128)(2,1)}, u32[]{:S(2)}) %copy-start) | copy-done | bytes 1572888
  43.2 3.3 %stack_pairs.1 = f32[6,8,2,128,128]{4,3,2,1,0:T(8,128)} custom-call(bf16[2,192,2048]{2,1,0:T(8,128)(2,1)S(1)} %copy-done), custom_call_target="tpu_custom_call" | custom-call | tf_op jit(solution)/shard_map/stack_pairs/pallas_call | solution.py:405
Async XLA Ops:
  41.8 1.4 %copy-start = (bf16[2,192,2048]{2,1,0:T(8,128)(2,1)S(1)}, bf16[2,192,2048]{2,1,0:T(8,128)(2,1)}, u32[]{:S(2)}) copy-start(bf16[2,192,2048]{2,1,0:T(8,128)(2,1)} %gather_picked.1.picked_ref) | copy-start | bytes 4718596

commit v5 on v2

--- a/solution.py
+++ b/solution.py
@@ -17,15 +17,12 @@
 
 
 def transform_table(length):
-    samples = jnp.arange(length, dtype=jnp.int32)
-    bin_index = FIRST_BIN + jnp.arange(BINS, dtype=jnp.int32)
-    phases = samples[:, None] * bin_index[None, :] % length
-    angles = 2.0 * math.pi / length * phases.astype(jnp.float32)
-    taper = 0.5 - 0.5 * jnp.cos(2.0 * math.pi / length * samples.astype(jnp.float32))
-    weight_col = (taper / math.sqrt(length))[:, None]
-    return jnp.concatenate(
-        [jnp.cos(angles) * weight_col, -jnp.sin(angles) * weight_col], axis=1
-    ).astype(jnp.bfloat16)
+    samples = np.arange(length)
+    phases = samples[None, :] * (FIRST_BIN + np.arange(BINS))[:, None] % length
+    angles = 2.0 * np.pi / length * phases
+    weight = (0.5 - 0.5 * np.cos(2.0 * np.pi / length * samples)) / math.sqrt(length)
+    rows = np.concatenate([np.cos(angles) * weight, -np.sin(angles) * weight])
+    return rows.astype(np.float32).astype(jnp.bfloat16)
 
 
 def gather_kernel(groups, pairs, blocks_ref, map_ref, table_ref, records_ref, picked_ref,
@@ -182,10 +179,11 @@
             pltpu.make_async_copy(maps.at[group], maps.at[group], map_recv.at[group]).wait()
         table = jnp.broadcast_to(maps[group], (WIN, total))
         for ref in range(2 * slots):
-            block = jnp.maximum(blocks_ref[0, ref // 2, ref % 2], 0)
+            block = blocks_ref[0, ref // 2, ref % 2]
             source = jnp.sum(
                 jnp.where(lane == wanted_lane + block, table, 0), axis=1, keepdims=True
             )
+            source = jnp.where(block >= 0, source, -1)
             for zz in range(depth):
                 hit = (column + zz * layer == source).astype(jnp.float32).astype(jnp.bfloat16)
                 onehot[group, zz, ref * WIN:(ref + 1) * WIN, :] = hit
@@ -306,54 +304,62 @@
     )(pair_blocks, source_map, table, records)
 
 
-def stack_kernel(groups, bins, channels, scale, blocks_ref, picked_ref, out_ref):
-    s = pl.program_id(0)
-    factor = jnp.where(blocks_ref[0, s, 0] >= 0, scale, 0.0).astype(jnp.float32)
-    for f in range(bins):
-        real = slice(f * channels, (f + 1) * channels)
-        imag = slice((bins + f) * channels, (bins + f + 1) * channels)
-        x_re = [picked_ref[g, :WIN, real] for g in range(groups)]
-        x_im = [picked_ref[g, :WIN, imag] for g in range(groups)]
-        y_re = jnp.concatenate([picked_ref[g, WIN:, real] for g in range(groups)], axis=0)
-        y_im = jnp.concatenate([picked_ref[g, WIN:, imag] for g in range(groups)], axis=0)
-        lhs = jnp.concatenate(x_re + x_im, axis=0)
-        rhs = jnp.concatenate(
-            [
-                jnp.concatenate([y_re, -y_im], axis=1),
-                jnp.concatenate([y_im, y_re], axis=1),
-            ],
-            axis=0,
-        )
-        both = lax.dot_general(lhs, rhs, (((0,), (0,)), ((), ())), preferred_element_type=jnp.float32)
-        out_ref[0, f, 0] = both[:, :channels] * factor
-        out_ref[0, f, 1] = both[:, channels:] * factor
-
-
-def stack_pairs(pair_blocks, picked, channels):
+def stack_kernel(groups, scale, picked_ref, out_ref, done, sems):
+    slots, bins, _, channels, _ = out_ref.shape
+
+    def write(s, f):
+        return pltpu.make_async_copy(done.at[s, f], out_ref.at[s, f], sems.at[s, f])
+
+    for s in range(slots):
+        left = slice(2 * s * WIN, (2 * s + 1) * WIN)
+        right = slice((2 * s + 1) * WIN, (2 * s + 2) * WIN)
+        for f in range(bins):
+            real = slice(f * channels, (f + 1) * channels)
+            imag = slice((bins + f) * channels, (bins + f + 1) * channels)
+            x_re = [picked_ref[g, left, real] for g in range(groups)]
+            x_im = [picked_ref[g, left, imag] for g in range(groups)]
+            y_re = jnp.concatenate([picked_ref[g, right, real] for g in range(groups)], axis=0)
+            y_im = jnp.concatenate([picked_ref[g, right, imag] for g in range(groups)], axis=0)
+            lhs = jnp.concatenate(x_re + x_im, axis=0)
+            rhs = jnp.concatenate(
+                [
+                    jnp.concatenate([y_re, -y_im], axis=1),
+                    jnp.concatenate([y_im, y_re], axis=1),
+                ],
+                axis=0,
+            )
+            both = lax.dot_general(
+                lhs, rhs, (((0,), (0,)), ((), ())), preferred_element_type=jnp.float32
+            )
+            done[s, f, 0] = both[:, :channels] * scale
+            done[s, f, 1] = both[:, channels:] * scale
+            write(s, f).start()
+    for s in range(slots):
+        for f in range(bins):
+            write(s, f).wait()
+
+
+def stack_pairs(slots, picked, channels):
     groups, _, width = picked.shape
-    slots = pair_blocks.shape[1]
     bins = width // (2 * channels)
     scale = 1.0 / math.sqrt(WIN * groups)
+    vmem = pl.BlockSpec(memory_space=pltpu.VMEM)
+    shape = (slots, bins, 2, channels, channels)
     return pl.pallas_call(
-        functools.partial(stack_kernel, groups, bins, channels, scale),
-        out_shape=jax.ShapeDtypeStruct((slots, bins, 2, channels, channels), jnp.float32),
-        grid=(slots,),
-        in_specs=[
-            pl.BlockSpec(memory_space=pltpu.SMEM),
-            pl.BlockSpec((groups, 2 * WIN, width), lambda s: (0, s, 0)),
-        ],
-        out_specs=pl.BlockSpec((1, bins, 2, channels, channels), lambda s: (s, 0, 0, 0, 0)),
-        compiler_params=pltpu.CompilerParams(
-            dimension_semantics=("arbitrary",), vmem_limit_bytes=40 << 20
-        ),
+        functools.partial(stack_kernel, groups, scale),
+        out_shape=jax.ShapeDtypeStruct(shape, jnp.float32),
+        in_specs=[vmem],
+        out_specs=pl.BlockSpec(memory_space=pl.ANY),
+        scratch_shapes=[pltpu.VMEM(shape, jnp.float32), pltpu.SemaphoreType.DMA((slots, bins))],
+        compiler_params=pltpu.CompilerParams(vmem_limit_bytes=40 << 20),
         name="stack_pairs",
-    )(pair_blocks, picked)
+    )(picked)
 
 
 def per_device(groups, pairs, records, source_map, pair_blocks):
-    table = transform_table(records.shape[3]).T
+    table = jnp.asarray(transform_table(records.shape[3]))
     picked = gather_picked(pair_blocks, source_map, table, records[0], groups, pairs)
-    return stack_pairs(pair_blocks, picked, records.shape[2])
+    return stack_pairs(pair_blocks.shape[1], picked, records.shape[2])
 
 
 def solution(mesh):

time: 46.3 us -> 44.8 us (0.968)
  Pallas kernels: 43.9 us -> 42.3 us
  local copies, waits for them, and re-layouts: 1.44 us -> 2.35 us
  other arithmetic: 0.68 us -> 0 us
    pallas_call x1, Pallas kernels: 4.94 us -> 3.27 us  [stack_pairs(): pl.pallas_call(functools.partial(stack_kernel, groups, scale), out_shape=...]
    unnamed x3 -> x5, local copies, waits for them, and re-layouts: 1.44 us -> 2.35 us
    another operation x1 -> x0, other arithmetic: 0.61 us -> none
where the time goes in v5:
time: 44.8 us; the launch traced here: 44.6 us
  Pallas kernels  42.3 us (94%)
  local copies, waits for them, and re-layouts  2.35 us (5%)
    pallas_call x1, Pallas kernels, gather_picked(): pl.pallas_call(functools.partial(gather_kernel, groups, pairs), out_shape...  39 us
    pallas_call x1, Pallas kernels, stack_pairs(): pl.pallas_call(functools.partial(stack_kernel, groups, scale), out_shape=...  3.27 us
    unnamed x5, local copies, waits for them, and re-layouts  2.35 us

profile of v5, /device:TPU:0, one launch (start us, length us, event | category | flops | bytes accessed | tf_op | source)
XLA Modules:
  0.0 44.6 jit_solution(5400468602983900993)
XLA Ops:
  0.0 0.8 %copy.5.blocks_ref = s32[1,6,2]{2,1,0:T(8,128)S(1)} copy(s32[1,6,2]{1,2,0:T(2,128)} %param.6) | data formatting | bytes 96 | tf_op args[2]
  0.8 0.0 copy-start
  0.8 0.9 %copy-done = bf16[32,2048]{1,0:T(8,128)(2,1)S(1)} copy-done((bf16[32,2048]{1,0:T(8,128)(2,1)S(1)}, bf16[32,2048]{1,0:T(8,128)(2,1)}, u32[]{:S(2)}) %copy-start) | copy-done | bytes 131096
  1.7 0.0 copy-start.1
  1.7 0.7 %copy-done.1 = s32[1,512]{1,0:T(1,128)S(1)} copy-done((s32[1,512]{1,0:T(1,128)S(1)}, s32[1,512]{1,0:T(1,128)}, u32[]{:S(2)}) %copy-start.1) | copy-done | bytes 2072
  2.4 39.0 %gather_picked.1.picked_ref = bf16[2,192,2048]{2,1,0:T(8,128)(2,1)S(1)} custom-call(s32[1,6,2]{2,1,0:T(8,128)S(1)} %copy.5.blocks_ref, s32[1,512]{1,0:T(1,128)S(1)} %copy-done.1, bf16[32,2048]{1,0:T(8,128)(2,1)S(1)} %copy-done, bf16[32,128,2048]{2,1,0:T(8,128)(2,1)} %bitcast.1), custom_call_target="tpu_custom_call" | custom-call | tf_op jit(solution)/shard_map/gather_picked/pallas_call | solution.py:275
  41.4 3.3 %stack_pairs.1 = f32[6,8,2,128,128]{4,3,2,1,0:T(8,128)} custom-call(bf16[2,192,2048]{2,1,0:T(8,128)(2,1)S(1)} %gather_picked.1.picked_ref), custom_call_target="tpu_custom_call" | custom-call | tf_op jit(solution)/shard_map/stack_pairs/pallas_call | solution.py:348
Async XLA Ops:
  0.8 0.9 %copy-start = (bf16[32,2048]{1,0:T(8,128)(2,1)S(1)}, bf16[32,2048]{1,0:T(8,128)(2,1)}, u32[]{:S(2)}) copy-start(bf16[32,2048]{1,0:T(8,128)(2,1)} %constant.2.clone.table_ref) | copy-start | bytes 393220
  1.7 0.7 %copy-start.1 = (s32[1,512]{1,0:T(1,128)S(1)}, s32[1,512]{1,0:T(1,128)}, u32[]{:S(2)}) copy-start(s32[1,512]{1,0:T(1,128)} %map_ref.1) | copy-start | bytes 6148
